TPU v7x, 32 devices: a whole 2x2x4 slice. The times are simulated.
32 devices in a mesh: dp: 8 (over y, x, core), tp: 4 (over z).
Axes of the slice: x: 2, y: 2, z: 4, core: 2. Of those that a mesh axis runs over, the one named last changes fastest.
Arguments:
- block_in: bfloat16 [128, 4, 37632], P('dp', 'tp'), may hold values from -6 to 6
- ln1_gain: float32 [768], P('tp'), may hold values from 0.1 to 1.9
- ln1_shift: float32 [768], P('tp'), may hold values from -1.75 to 1.75
- tok_w1: float32 [196, 384], replicated, may hold values from -0.4375 to 0.4375
- tok_b1: float32 [384], replicated, may hold values from -1.75 to 1.75
- tok_w2: float32 [384, 196], replicated, may hold values from -0.3125 to 0.3125
- tok_b2: float32 [196], replicated, may hold values from -1.75 to 1.75
- ln2_gain: float32 [768], P('tp'), may hold values from 0.1 to 1.9
- ln2_shift: float32 [768], P('tp'), may hold values from -1.75 to 1.75
- ch_w1: float32 [768, 3072], P('dp', 'tp'), may hold values from -0.21875 to 0.21875
- ch_b1: float32 [3072], replicated, may hold values from -1.75 to 1.75
- ch_w2: float32 [3072, 768], P('tp', 'dp'), may hold values from -0.109375 to 0.109375
- ch_b2: float32 [768], replicated, may hold values from -1.75 to 1.75
- group_ids: int32 [128], P('dp'), may hold values from 0 to 63
- out_grad: bfloat16 [128, 4, 37632], P('dp', 'tp'), may hold values from -6 to 6
Outputs:
- block_out: bfloat16 [128, 4, 37632], P('dp', 'tp')
- dx: bfloat16 [128, 4, 37632], P('dp', 'tp')
- group_norms: float32 [64], replicated
- d_ln1_gain: float32 [768], P('tp')
- d_ln1_shift: float32 [768], P('tp')
- d_tok_w1: float32 [196, 384], replicated
- d_tok_b1: float32 [384], replicated
- d_tok_w2: float32 [384, 196], replicated
- d_tok_b2: float32 [196], replicated
- d_ln2_gain: float32 [768], P('tp')
- d_ln2_shift: float32 [768], P('tp')
- d_ch_w1: float32 [768, 3072], P('dp', 'tp')
- d_ch_b1: float32 [3072], replicated
- d_ch_w2: float32 [3072, 768], P('tp', 'dp')
- d_ch_b2: float32 [768], replicated
All inputs are finite; a program needn't handle non-finite values.
Results may differ from a plain program's by a relative error of at most 0.01.
Values may be sent and summed in bfloat16 or wider, within the bound.
A program may use at most 128 MiB of HBM per device.

v0:
```python
import math
import jax
import jax.numpy as jnp
from jax import lax
from jax.sharding import PartitionSpec as P

S = 196
GROUPS = 64
epsilon = 1e-06
highest = lax.Precision.HIGHEST


def in_blocks(array, dim, size):
    lengths = array.shape
    tiles = array.reshape(*lengths[:dim], size, lengths[dim] // size, *lengths[dim + 1 :])
    return jnp.moveaxis(tiles, dim, 0)


def sum_at_owner(array, axis, dim):
    size = lax.axis_size(axis)
    tiles = lax.all_to_all(in_blocks(array, dim, size), axis, 0, 0, tiled=True)
    return jnp.sum(tiles.astype(jnp.float32), axis=0)


def norm_stats(values, full_width):
    totals = lax.psum((jnp.sum(values, -1), jnp.sum(values * values, -1)), "tp")
    average = totals[0] / full_width
    inverse = lax.rsqrt(totals[1] / full_width - average * average + epsilon)
    return ((values - average[..., None]) * inverse[..., None], inverse)


def norm_back(grad_hat, normed, inverse, full_width):
    totals = lax.psum((jnp.sum(grad_hat, -1), jnp.sum(grad_hat * normed, -1)), "tp")
    return inverse[..., None] * (
        grad_hat - totals[0][..., None] / full_width - normed * totals[1][..., None] / full_width
    )


def spread_slot(values, slot_mask):
    expanded = values[..., None, :] * slot_mask[:, None]
    return expanded.reshape(values.shape[:-1] + (slot_mask.shape[0] * values.shape[-1],))


def gather_channels(values):
    return lax.all_gather(values, "tp", axis=1, tiled=True)


def sum_channels(values):
    return lax.psum_scatter(
        values.astype(jnp.bfloat16), "tp", scatter_dimension=1, tiled=True
    ).astype(jnp.float32)


def per_device(
    block_in,
    ln1_gain,
    ln1_shift,
    tok_w1,
    tok_b1,
    tok_w2,
    tok_b2,
    ln2_gain,
    ln2_shift,
    ch_w1,
    ch_b1,
    ch_w2,
    ch_b2,
    group_ids,
    out_grad,
):
    f32 = jnp.float32
    bf16 = jnp.bfloat16
    images = block_in.shape[0]
    patches = S
    plain_in = block_in.reshape(images, patches, -1)
    plain_grad = out_grad.reshape(images, patches, -1)
    local_width = plain_in.shape[2]
    tp_count = lax.axis_size("tp")
    dp_count = lax.axis_size("dp")
    tp_place = lax.axis_index("tp")
    full_width = local_width * tp_count
    slot_mask = (jnp.arange(tp_count) == tp_place).astype(f32)
    row_count = images * patches
    input_float = plain_in.astype(f32)
    normed_one, inverse_one = norm_stats(input_float, full_width)
    mixed_in = (normed_one * ln1_gain + ln1_shift).astype(bf16)
    token_w1 = tok_w1.astype(bf16)
    token_w2 = tok_w2.astype(bf16)
    pre_act = jnp.einsum("nsc,sk->nck", mixed_in, token_w1, preferred_element_type=f32) + tok_b1
    hidden_act, gelu_token = jax.vjp(jax.nn.gelu, pre_act)
    hidden_low = hidden_act.astype(bf16)
    token_out = (
        jnp.einsum("nck,ks->nsc", hidden_low, token_w2, preferred_element_type=f32)
        + tok_b2[None, :, None]
    )
    residual = input_float + token_out
    normed_two, inverse_two = norm_stats(residual, full_width)
    branch_in = (normed_two * ln2_gain + ln2_shift).astype(bf16).reshape(row_count, local_width)
    grad_low = plain_grad.reshape(row_count, local_width)
    upper_rows, lower_rows = (
        lax.all_gather(ch_w1.astype(bf16), "dp", axis=0, tiled=True),
        lax.all_gather(ch_w2.astype(bf16), "dp", axis=1, tiled=True),
    )
    gathered = gather_channels(branch_in)
    hidden_width = upper_rows.shape[1]
    bias_first = lax.dynamic_slice_in_dim(ch_b1, tp_place * hidden_width, hidden_width)
    bias_second = lax.dynamic_slice_in_dim(ch_b2, tp_place * local_width, local_width)
    inner_act = jnp.dot(gathered, upper_rows, preferred_element_type=f32) + bias_first
    activated, gelu_branch = jax.vjp(jax.nn.gelu, inner_act)
    activated_low = activated.astype(bf16)
    branch_sum = (
        sum_channels(jnp.dot(activated_low, lower_rows, preferred_element_type=f32)) + bias_second
    )
    branch_low = branch_sum.astype(bf16)
    grad_full = gather_channels(grad_low)
    grad_activated = jnp.dot(grad_full, lower_rows.T, preferred_element_type=f32)
    grad_lower = jnp.dot(activated_low.T, grad_full, preferred_element_type=f32)
    grad_inner = gelu_branch(grad_activated)[0].astype(bf16)
    grad_upper = jnp.dot(gathered.T, grad_inner, preferred_element_type=f32)
    bias_first_grad = spread_slot(jnp.sum(grad_inner.astype(f32), 0), slot_mask)
    bias_second_grad = spread_slot(jnp.sum(grad_low.astype(f32), 0), slot_mask)
    grad_branch = sum_channels(jnp.dot(grad_inner, upper_rows.T, preferred_element_type=f32))
    upper_grad, lower_grad = (
        sum_at_owner(grad_upper.astype(jnp.bfloat16), "dp", 0),
        sum_at_owner(grad_lower.astype(jnp.bfloat16), "dp", 1),
    )
    output = (residual + branch_low.astype(f32).reshape(residual.shape)).astype(bf16)
    grad_normed = grad_branch.reshape(residual.shape)
    image_gain = jnp.sum(grad_normed * normed_two, 1)
    image_shift = jnp.sum(grad_normed, 1)
    grad_resid = plain_grad.astype(f32) + norm_back(
        grad_normed * ln2_gain, normed_two, inverse_two, full_width
    )
    grad_token_low = grad_resid.astype(bf16)
    grad_hidden = jnp.einsum("nsc,ks->nck", grad_token_low, token_w2, preferred_element_type=f32)
    token_w2_grad = jnp.einsum(
        "nck,nsc->ks", hidden_low, grad_token_low, preferred_element_type=f32
    )
    token_b2_grad = jnp.sum(grad_token_low.astype(f32), (0, 2))
    grad_pre = gelu_token(grad_hidden)[0].astype(bf16)
    token_w1_grad = jnp.einsum("nsc,nck->sk", mixed_in, grad_pre, preferred_element_type=f32)
    token_b1_grad = jnp.sum(grad_pre.astype(f32), (0, 1))
    grad_mixed = jnp.einsum("nck,sk->nsc", grad_pre, token_w1, preferred_element_type=f32)
    gain_one_grad = jnp.sum(grad_mixed * normed_one, (0, 1))
    shift_one_grad = jnp.sum(grad_mixed, (0, 1))
    grad_input = (
        grad_resid + norm_back(grad_mixed * ln1_gain, normed_one, inverse_one, full_width)
    ).astype(bf16)
    member = (group_ids[:, None] == jnp.arange(GROUPS)[None, :]).astype(f32)
    image_stats = jnp.stack([image_gain, image_shift], 1).reshape(images, 2 * local_width)
    group_local = jnp.dot(member.T, image_stats, precision=highest).reshape(GROUPS, 2, local_width)
    norm_one_local = jnp.stack([gain_one_grad, shift_one_grad], 0)
    totals = lax.psum(
        (
            token_w1_grad,
            token_b1_grad,
            token_w2_grad,
            token_b2_grad,
            spread_slot(group_local, slot_mask),
            spread_slot(norm_one_local, slot_mask),
            bias_first_grad,
            bias_second_grad,
        ),
        ("dp", "tp"),
    )
    group_full = totals[4]
    group_norms = jnp.sqrt(jnp.sum(group_full * group_full, (1, 2)))
    clip_bound = 2.0 * math.sqrt(images * dp_count * patches * full_width / GROUPS)
    factor = clip_bound / jnp.maximum(group_norms, clip_bound)
    clipped = jnp.sum(factor[:, None, None] * group_full, 0)
    clipped_local = lax.dynamic_slice_in_dim(clipped, tp_place * local_width, local_width, 1)
    norm_one_own = lax.dynamic_slice_in_dim(totals[5], tp_place * local_width, local_width, 1)
    stored_out = output.reshape(images, 1, patches * local_width)
    stored_grad = grad_input.reshape(images, 1, patches * local_width)
    return (
        stored_out,
        stored_grad,
        group_norms,
        norm_one_own[0],
        norm_one_own[1],
        totals[0],
        totals[1],
        totals[2],
        totals[3],
        clipped_local[0],
        clipped_local[1],
        upper_grad,
        totals[6],
        lower_grad,
        totals[7],
    )


def solution(mesh):
    in_specs = (
        P("dp", "tp", None),
        P("tp"),
        P("tp"),
        P(),
        P(),
        P(),
        P(),
        P("tp"),
        P("tp"),
        P("dp", "tp"),
        P(),
        P("tp", "dp"),
        P(),
        P("dp"),
        P("dp", "tp", None),
    )
    out_specs = (
        P("dp", "tp", None),
        P("dp", "tp", None),
        P(),
        P("tp"),
        P("tp"),
        P(),
        P(),
        P(),
        P(),
        P("tp"),
        P("tp"),
        P("dp", "tp"),
        P(),
        P("tp", "dp"),
        P(),
    )
    return jax.shard_map(
        per_device, mesh=mesh, in_specs=in_specs, out_specs=out_specs, check_vma=False
    )
```

profile of v0, /device:TPU:0, one launch (start us, length us, event | category | flops | bytes accessed | tf_op | source)
XLA Modules:
  0.0 688.9 jit_solution(15931302584527314932)
XLA Ops:
  15.6 20.9 %all-reduce.5 = (f32[16,196]{1,0:T(8,128)S(1)}, f32[16,196]{1,0:T(8,128)S(1)}) all-reduce(f32[16,196]{1,0:T(8,128)S(1)} %get-tuple-element.20, f32[16,196]{1,0:T(8,128)S(1)} %get-tuple-element.19), channel_id=1, replica_groups=mesh['dp'=8,'tp'=4] {'tp'}, use_global_device_ids=true, to_apply=%region_3.0 | all-reduce | flops 6272 | bytes 50176 | tf_op jit(solution)/shard_map/psum | solution.py:26
  44.6 15.8 %all-reduce.4 = (f32[16,196]{1,0:T(8,128)S(1)}, f32[16,196]{1,0:T(8,128)S(1)}) all-reduce(f32[16,196]{1,0:T(8,128)S(1)} %get-tuple-element.23, f32[16,196]{1,0:T(8,128)S(1)} %get-tuple-element.22), channel_id=1, replica_groups=mesh['dp'=8,'tp'=4] {'tp'}, use_global_device_ids=true, to_apply=%region_7.0 | all-reduce | flops 6272 | bytes 50176 | tf_op jit(solution)/shard_map/psum | solution.py:26
  76.0 84.4 %all-gather.5.cloned.1.call-done = bf16[3136,768]{0,1:T(8,128)(2,1)} async-done(((bf16[3136,192]{0,1:T(8,128)(2,1)}), bf16[3136,768]{0,1:T(8,128)(2,1)}) %all-gather.5.cloned.1.call-update) | async-done | bytes 4816912 | tf_op jit(solution)/shard_map/all_gather | solution.py:45
  160.4 10.4 %fusion.40 = f32[3136,768]{1,0:T(8,128)} fusion(bf16[3136,768]{0,1:T(8,128)(2,1)} %all-gather.5.cloned.1.call-done, bf16[768,768]{1,0:T(8,128)(2,1)} %all-gather.7.cloned.1.call-done), kind=kOutput, calls=%fused_computation.92 | convolution fusion | flops 3699376128 | bytes 15630336 | tf_op jit(solution)/shard_map/dot_general | solution.py:108
  170.8 14.6 %all-gather.9.cloned.1.call-done = bf16[768,768]{0,1:T(8,128)(2,1)} async-done(((bf16[768,96]{0,1:T(8,128)(2,1)}), bf16[768,768]{0,1:T(8,128)(2,1)}) %all-gather.9.cloned.1.call-update) | async-done | bytes 1179664 | tf_op jit(solution)/shard_map/all_gather | solution.py:102
  185.4 10.6 %convolution_convert_fusion.1 = bf16[3136,768]{0,1:T(8,128)(2,1)} fusion(bf16[768,768]{0,1:T(8,128)(2,1)} %all-gather.9.cloned.1.call-done, f32[3136,768]{1,0:T(8,128)} %fusion.40, f32[768]{0:T(1024)S(1)} %dynamic_slice.12), kind=kOutput, calls=%fused_computation.14 | convolution fusion | flops 3725869056 | bytes 15633408 | tf_op jit(solution)/shard_map/dot_general | solution.py:112
  196.4 83.0 %all-gather.11.cloned.1.call-done = bf16[3136,768]{0,1:T(8,128)(2,1)} async-done(((bf16[3136,192]{0,1:T(8,128)(2,1)}), bf16[3136,768]{0,1:T(8,128)(2,1)}) %all-gather.11.cloned.1.call-update) | async-done | bytes 4816912 | tf_op jit(solution)/shard_map/all_gather | solution.py:45
  279.5 15.2 %convert_reduce_fusion = (f32[768]{0:T(1024)S(1)}, bf16[3136,768]{1,0:T(8,128)(2,1)S(1)}) fusion(f32[3136,768]{1,0:T(8,128)} %fusion.40, f32[768]{0:T(1024)S(1)} %dynamic_slice.12, bf16[3136,768]{0,1:T(8,128)(2,1)} %all-gather.11.cloned.1.call-done, bf16[768,768]{0,1:T(8,128)(2,1)} %all-gather.9.cloned.1.call-done), kind=kOutput, calls=%fused_computation.9 | convolution fusion | flops 3754769664 | bytes 20453376 | tf_op jit(solution)/shard_map/dot_general | solution.py:116
  296.8 5.9 convolution_convert_fusion
  302.7 10.6 %convolution_convert_fusion.2 = bf16[768,768]{0,1:T(8,128)(2,1)} fusion(bf16[3136,768]{0,1:T(8,128)(2,1)} %all-gather.11.cloned.1.call-done, f32[3136,768]{1,0:T(8,128)} %fusion.40, f32[768]{0:T(1024)S(1)} %dynamic_slice.12), kind=kOutput, calls=%fused_computation.49 | convolution fusion | flops 3724050432 | bytes 15633408 | tf_op jit(solution)/shard_map/dot_general | solution.py:117
  317.8 9.1 %convolution_convert_fusion.3 = bf16[768,768]{1,0:T(8,128)(2,1)} fusion(bf16[3136,768]{0,1:T(8,128)(2,1)} %all-gather.5.cloned.1.call-done, bf16[3136,768]{1,0:T(8,128)(2,1)} %copy-done.29), kind=kOutput, calls=%fused_computation.50 | convolution fusion | flops 3699965952 | bytes 10813440 | tf_op jit(solution)/shard_map/dot_general | solution.py:119
  326.9 7.7 %all-to-all-done.1 = bf16[8,768,96]{1,2,0:T(8,128)(2,1)} async-done(((bf16[8,768,96]{1,2,0:T(8,128)(2,1)}), bf16[8,768,96]{1,2,0:T(8,128)(2,1)}, u32[]{:S(2)}, u32[]{:S(2)}) %all-to-all-start.1) | async-done | bytes 1179680 | tf_op jit(solution)/shard_map/all_to_all | solution.py:21
  341.9 4.8 copy.76
  357.9 10.7 %reduce-scatter.3.cloned.1.call-done = bf16[3136,192]{0,1:T(8,128)(2,1)} async-done(((bf16[3136,768]{0,1:T(8,128)(2,1)}), bf16[3136,192]{0,1:T(8,128)(2,1)}) %reduce-scatter.3.cloned.1.call-update) | async-done | bytes 1204240 | tf_op jit(solution)/shard_map/reduce_scatter | solution.py:49
  370.1 5.7 reshape.138
  375.8 84.1 %reduce-scatter.5.cloned.1.call-done = bf16[3136,192]{0,1:T(8,128)(2,1)} async-done(((bf16[3136,768]{0,1:T(8,128)(2,1)}), bf16[3136,192]{0,1:T(8,128)(2,1)}) %reduce-scatter.5.cloned.1.call-update) | async-done | bytes 1204240 | tf_op jit(solution)/shard_map/reduce_scatter | solution.py:49
  462.2 5.7 reshape.130
  472.7 19.7 %all-reduce.3 = (f32[16,196]{1,0:T(8,128)}, f32[16,196]{1,0:T(8,128)}) all-reduce(f32[16,196]{1,0:T(8,128)S(1)} %get-tuple-element.18, f32[16,196]{1,0:T(8,128)} %reduce_sum.187), channel_id=1, replica_groups=mesh['dp'=8,'tp'=4] {'tp'}, use_global_device_ids=true, to_apply=%region_13.0 | all-reduce | flops 6272 | bytes 50176 | tf_op jit(solution)/shard_map/psum | solution.py:33
  493.1 8.6 %convert_reduce_fusion.3 = (f32[196]{0:T(256)}, f32[16,196,192]{1,2,0:T(8,128)S(1)}, bf16[16,196,192]{1,2,0:T(8,128)(2,1)}) fusion(f32[16,196,192]{1,2,0:T(8,128)} %copy.76, f32[16,196]{1,0:T(8,128)} %get-tuple-element.34, f32[16,196,192]{1,2,0:T(8,128)} %copy-done.3, f32[16,196]{1,0:T(8,128)S(1)} %get-tuple-element.47, ...), kind=kLoop, calls=%fused_computation.32 | loop fusion | flops 8429372 | bytes 13298192 | tf_op jit(solution)/shard_map/reduce_sum | solution.py:139
  501.7 6.2 convolution_bitcast_fusion
  528.8 16.1 %all-reduce.2 = (f32[16,196]{1,0:T(8,128)S(1)}, f32[16,196]{1,0:T(8,128)S(1)}) all-reduce(f32[16,196]{1,0:T(8,128)S(1)} %get-tuple-element.16, f32[16,196]{1,0:T(8,128)S(1)} %get-tuple-element.21), channel_id=1, replica_groups=mesh['dp'=8,'tp'=4] {'tp'}, use_global_device_ids=true, to_apply=%region_17.0 | all-reduce | flops 6272 | bytes 50176 | tf_op jit(solution)/shard_map/psum | solution.py:33
  544.9 5.3 add_convert_fusion
  555.6 39.9 %all-reduce = (f32[2,768]{1,0:T(2,128)S(1)}, f32[384]{0:T(512)}, f32[196]{0:T(256)}, f32[3072]{0:T(1024)}, f32[768]{0:T(1024)}) all-reduce(f32[2,768]{1,0:T(2,128)S(1)} %broadcast_multiply_fusion.6, f32[384]{0:T(512)S(1)} %copy-done.19, f32[196]{0:T(256)S(1)} %copy-done.18, ...), channel_id=1, replica_groups=mesh['dp'=8,'tp'=4] {'dp','tp'}, use_global_device_ids=true, to_apply=%region_24.0 | all-reduce | flops 5956 | bytes 47648 | tf_op jit(solution)/shard_map/psum | solution.py:153
  595.5 79.3 %all-reduce.8.cloned.1.call-done = (f32[64,2,768]{2,0,1:T(8,128)}, f32[196,384]{1,0:T(8,128)}, f32[384,196]{0,1:T(8,128)}) async-done(((f32[64,2,768]{2,0,1:T(8,128)}, f32[196,384]{1,0:T(8,128)}, f32[384,196]{0,1:T(8,128)}), (f32[64,2,768]{2,0,1:T(8,128)}, f32[196,384]{1,0:T(8,128)}, f32[384,196]{0,1:T(8,128)})) %all-reduce.8.cloned.1.call-update) | async-done | bytes 995344 | tf_op jit(solution)/shard_map/psum | solution.py:153
  (146 shorter events, 99.7 us)
Async XLA Ops:
  7.2 68.8 %all-gather.7.cloned.1.call-start = ((), (), s32[]{:S(2)}) async-start(), calls=%async_computation.5 | async-start | bytes 1327104 | tf_op jit(solution)/shard_map/all_gather | solution.py:101
  8.9 151.5 %all-gather.5.cloned.1.call-start = ((), (), s32[]{:S(2)}) async-start(), calls=%async_computation.4 | async-start | bytes 6144000 | tf_op jit(solution)/shard_map/all_gather | solution.py:45
  12.3 24.2 %copy-start.15 = (f32[192]{0:T(256)S(1)}, f32[192]{0:T(256)}, u32[]{:S(2)}) copy-start(f32[192]{0:T(256)} %param.16) | copy-start | bytes 2308
  12.3 24.2 %copy-start.20 = (f32[192]{0:T(256)S(1)}, f32[192]{0:T(256)}, u32[]{:S(2)}) copy-start(f32[192]{0:T(256)} %param.17) | copy-start | bytes 2308
  15.6 24.6 %copy-start.10 = (f32[196,384]{1,0:T(8,128)S(1)}, f32[196,384]{1,0:T(8,128)}, u32[]{:S(2)}) copy-start(f32[196,384]{1,0:T(8,128)} %param.18) | copy-start | bytes 903172
  42.1 18.4 %copy-start.13 = (f32[192]{0:T(256)S(1)}, f32[192]{0:T(256)}, u32[]{:S(2)}) copy-start(f32[192]{0:T(256)} %param.22) | copy-start | bytes 2308
  44.6 19.2 %copy-start.3 = (f32[16,196,192]{1,2,0:T(8,128)}, f32[16,196,192]{1,2,0:T(8,128)S(1)}, u32[]{:S(2)}) copy-start(f32[16,196,192]{1,2,0:T(8,128)S(1)} %get-tuple-element.55) | copy-start | bytes 7225348
  68.1 117.2 %all-gather.9.cloned.1.call-start = ((), (), s32[]{:S(2)}) async-start(), calls=%async_computation.6 | async-start | bytes 1327104 | tf_op jit(solution)/shard_map/all_gather | solution.py:102
  69.8 209.6 %all-gather.11.cloned.1.call-start = ((), (), s32[]{:S(2)}) async-start(), calls=%async_computation.8 | async-start | bytes 6144000 | tf_op jit(solution)/shard_map/all_gather | solution.py:45
  74.9 293.6 %reduce-scatter.3.cloned.1.call-start = ((), (), s32[]{:S(2)}) async-start(), calls=%async_computation.7 | async-start | bytes 6144000 | tf_op jit(solution)/shard_map/reduce_scatter | solution.py:49
  196.0 100.9 %copy-start.23 = (bf16[768,768]{1,0:T(8,128)(2,1)S(1)}, bf16[768,768]{1,0:T(8,128)(2,1)}, u32[]{:S(2)}) copy-start(bf16[768,768]{1,0:T(8,128)(2,1)} %all-gather.7.cloned.1.call-done) | copy-start | bytes 3538948
  196.0 263.8 %reduce-scatter.5.cloned.1.call-start = ((), (), s32[]{:S(2)}) async-start(), calls=%async_computation.9 | async-start | bytes 6144000 | tf_op jit(solution)/shard_map/reduce_scatter | solution.py:49
  313.3 21.3 %all-to-all-start.1 = ((bf16[8,768,96]{1,2,0:T(8,128)(2,1)}), bf16[8,768,96]{1,2,0:T(8,128)(2,1)}, u32[]{:S(2)}, u32[]{:S(2)}) async-start(bf16[8,768,96]{1,2,0:T(8,128)(2,1)} %bitcast.18), calls=%async_computation.3 | async-start | bytes 2359296 | tf_op jit(solution)/shard_map/all_to_all | solution.py:21
  326.8 12.1 %copy-start.8 = (bf16[16,1,37632]{2,0,1:T(8,128)(2,1)S(1)}, bf16[16,1,37632]{2,0,1:T(8,128)(2,1)}, u32[]{:S(2)}) copy-start(bf16[16,1,37632]{2,0,1:T(8,128)(2,1)} %param.29) | copy-start | bytes 3612676
  334.6 21.1 %all-to-all-start = ((bf16[8,96,768]{2,1,0:T(8,128)(2,1)}), bf16[8,96,768]{2,1,0:T(8,128)(2,1)}, u32[]{:S(2)}, u32[]{:S(2)}) async-start(bf16[8,96,768]{2,1,0:T(8,128)(2,1)} %bitcast.81), calls=%async_computation.2 | async-start | bytes 2359296 | tf_op jit(solution)/shard_map/all_to_all | solution.py:21
  338.9 335.9 %all-reduce.8.cloned.1.call-start = ((), (), s32[]{:S(2)}) async-start(), calls=%async_computation.10 | async-start | bytes 2015232 | tf_op jit(solution)/shard_map/psum | solution.py:153
  370.0 89.8 %copy-start.14 = (f32[192]{0:T(256)S(1)}, f32[192]{0:T(256)}, u32[]{:S(2)}) copy-start(f32[192]{0:T(256)} %param.22) | copy-start | bytes 2308
  493.1 8.6 %copy-start.27 = (f32[384]{0:T(512)S(1)}, f32[384]{0:T(512)}, u32[]{:S(2)}) copy-start(f32[384]{0:T(512)} %param.19) | copy-start | bytes 4612
  493.1 14.8 %slice-start = ((s8[4718592]{0:T(1024)(128)(4,1)}), s8[4194304]{0:T(1024)(128)(4,1)S(1)}, s32[]{:S(2)}) async-start(s8[4718592]{0:T(1024)(128)(4,1)} %bitcast.79), calls=%async_computation.11 | async-start | bytes 8388608
  501.7 6.2 copy-start.4
  501.7 6.2 slice-start.1
  501.7 6.2 copy-start.25
  523.0 22.0 %copy-start.2 = (f32[16,196,192]{1,2,0:T(8,128)S(1)}, f32[16,196,192]{1,2,0:T(8,128)}, u32[]{:S(2)}) copy-start(f32[16,196,192]{1,2,0:T(8,128)} %copy.70) | copy-start | bytes 7225348
  523.0 22.0 %copy-start.17 = (f32[192]{0:T(256)S(1)}, f32[192]{0:T(256)}, u32[]{:S(2)}) copy-start(f32[192]{0:T(256)} %param.16) | copy-start | bytes 2308
  (17 other events, 51.9 us)
Sparse Core Ops, SparseCore 0:
  10.5 26.7 all-gather.6
  68.2 92.0 all-gather.4
  162.8 22.4 all-gather.8
  186.8 92.6 all-gather.10
  281.6 86.8 reduce-scatter.2
  370.8 88.9 reduce-scatter.4
  545.0 129.7 all-reduce.7
where the time goes:
time: 698 us; the launch traced here: 689 us
  waiting for transfers between devices  369 us (53%)
  blocking collectives  112 us (16%)
  matrix products  81.5 us (12%)
  local copies, waits for them, and re-layouts  59.5 us (9%)
  other arithmetic  42.3 us (6%)
  between operations  15 us (2%)
  starting transfers between devices  9.6 us (1%)
    all_gather x2, waiting for transfers between devices, gather_channels(): return lax.all_gather(values, 'tp', axis=1, tiled=True)  167 us
    reduce_scatter x2, waiting for transfers between devices, sum_channels(): lax.psum_scatter(values.astype(jnp.bfloat16), 'tp', scatter_dimension=1,...  94.7 us
    psum x1, waiting for transfers between devices, per_device(): lax.psum((token_w1_grad, token_b1_grad, token_w2_grad, token_b2_grad, spr...  79.3 us
    psum x1, blocking collectives, per_device(): lax.psum((token_w1_grad, token_b1_grad, token_w2_grad, token_b2_grad, spr...  39.9 us
    psum x2, blocking collectives, norm_stats(): totals = lax.psum((jnp.sum(values, -1), jnp.sum(values * values, -1)), 'tp')  36.8 us
    psum x2, blocking collectives, norm_back(): lax.psum((jnp.sum(grad_hat, -1), jnp.sum(grad_hat * normed, -1)), 'tp')  35.7 us
    dot_general x1, matrix products, per_device(): jnp.dot(grad_full, lower_rows.T, preferred_element_type=f32)  15.2 us
    all_gather x1, waiting for transfers between devices, per_device(): lax.all_gather(ch_w2.astype(bf16), 'dp', axis=1, tiled=True)  14.6 us
  transfers between devices with their start and end apart: 9, of which 8 were waited for; matrix products, arithmetic and copies ran while one was open for 18% of the time, Pallas kernels for 0%

commit v1 on v0

--- a/solution.py
+++ b/solution.py
@@ -151,17 +151,20 @@
     group_local = jnp.dot(member.T, image_stats, precision=highest).reshape(GROUPS, 2, local_width)
     norm_one_local = jnp.stack([gain_one_grad, shift_one_grad], 0)
     totals = lax.psum(
-        (
-            token_w1_grad,
-            token_b1_grad,
-            token_w2_grad,
-            token_b2_grad,
-            spread_slot(group_local, slot_mask),
-            spread_slot(norm_one_local, slot_mask),
-            bias_first_grad,
-            bias_second_grad,
+        lax.psum(
+            (
+                token_w1_grad,
+                token_b1_grad,
+                token_w2_grad,
+                token_b2_grad,
+                spread_slot(group_local, slot_mask),
+                spread_slot(norm_one_local, slot_mask),
+                bias_first_grad,
+                bias_second_grad,
+            ),
+            "tp",
         ),
-        ("dp", "tp"),
+        "dp",
     )
     group_full = totals[4]
     group_norms = jnp.sqrt(jnp.sum(group_full * group_full, (1, 2)))

time: 698 us -> 662 us (0.948)
  waiting for transfers between devices: 369 us -> 339 us
  blocking collectives: 112 us -> 99.5 us
    psum x1, waiting for transfers between devices: 79.3 us -> 25.5 us  [per_device(): lax.psum((token_w1_grad, token_b1_grad, token_w2_grad, token_b2_grad, spr...]
    psum x0 -> x1, waiting for transfers between devices: none -> 24.6 us  [per_device(): lax.psum(lax.psum((token_w1_grad, token_b1_grad, token_w2_grad, token_b2_...]
    psum x1, blocking collectives: 39.9 us -> 24.9 us  [per_device(): lax.psum(lax.psum((token_w1_grad, token_b1_grad, token_w2_grad, token_b2_...]
  transfers between devices with their start and end apart: 9 -> 10, of which waited for: 8 -> 9; matrix products, arithmetic and copies ran while one was open for 18% -> 20% of each run, Pallas kernels for 0% -> 0%
where the time goes in v1:
time: 662 us; the launch traced here: 653 us
  waiting for transfers between devices  339 us (51%)
  blocking collectives  99.5 us (15%)
  matrix products  86.3 us (13%)
  local copies, waits for them, and re-layouts  60.2 us (9%)
  other arithmetic  42.8 us (6%)
  between operations  15.1 us (2%)
  starting transfers between devices  9.64 us (1%)
    all_gather x2, waiting for transfers between devices, gather_channels(): return lax.all_gather(values, 'tp', axis=1, tiled=True)  167 us
    reduce_scatter x2, waiting for transfers between devices, sum_channels(): lax.psum_scatter(values.astype(jnp.bfloat16), 'tp', scatter_dimension=1,...  94.7 us
    psum x2, blocking collectives, norm_stats(): totals = lax.psum((jnp.sum(values, -1), jnp.sum(values * values, -1)), 'tp')  37.4 us
    psum x2, blocking collectives, norm_back(): lax.psum((jnp.sum(grad_hat, -1), jnp.sum(grad_hat * normed, -1)), 'tp')  37.1 us
    psum x1, waiting for transfers between devices, per_device(): lax.psum((token_w1_grad, token_b1_grad, token_w2_grad, token_b2_grad, spr...  25.5 us
    psum x1, blocking collectives, per_device(): lax.psum(lax.psum((token_w1_grad, token_b1_grad, token_w2_grad, token_b2_...  24.9 us
    psum x1, waiting for transfers between devices, per_device(): lax.psum(lax.psum((token_w1_grad, token_b1_grad, token_w2_grad, token_b2_...  24.6 us
    dot_general x1, matrix products, per_device(): jnp.dot(grad_full, lower_rows.T, preferred_element_type=f32)  15.2 us
  transfers between devices with their start and end apart: 10, of which 9 were waited for; matrix products, arithmetic and copies ran while one was open for 20% of the time, Pallas kernels for 0%

profile of v1, /device:TPU:0, one launch (start us, length us, event | category | flops | bytes accessed | tf_op | source)
XLA Modules:
  0.0 652.9 jit_solution(9838611191693056481)
XLA Ops:
  16.1 21.5 %all-reduce.5 = (f32[16,196]{1,0:T(8,128)S(1)}, f32[16,196]{1,0:T(8,128)S(1)}) all-reduce(f32[16,196]{1,0:T(8,128)} %get-tuple-element.20, f32[16,196]{1,0:T(8,128)} %get-tuple-element.19), channel_id=1, replica_groups=mesh['dp'=8,'tp'=4] {'tp'}, use_global_device_ids=true, to_apply=%region_3.0 | all-reduce | flops 6272 | bytes 50176 | tf_op jit(solution)/shard_map/psum | solution.py:26
  46.4 15.9 %all-reduce.4 = (f32[16,196]{1,0:T(8,128)S(1)}, f32[16,196]{1,0:T(8,128)S(1)}) all-reduce(f32[16,196]{1,0:T(8,128)S(1)} %get-tuple-element.23, f32[16,196]{1,0:T(8,128)S(1)} %get-tuple-element.22), channel_id=1, replica_groups=mesh['dp'=8,'tp'=4] {'tp'}, use_global_device_ids=true, to_apply=%region_7.0 | all-reduce | flops 6272 | bytes 50176 | tf_op jit(solution)/shard_map/psum | solution.py:26
  77.1 84.4 %all-gather.5.cloned.1.call-done = bf16[3136,768]{0,1:T(8,128)(2,1)} async-done(((bf16[3136,192]{0,1:T(8,128)(2,1)}), bf16[3136,768]{0,1:T(8,128)(2,1)}) %all-gather.5.cloned.1.call-update) | async-done | bytes 4816912 | tf_op jit(solution)/shard_map/all_gather | solution.py:45
  161.5 10.4 %fusion.40 = f32[3136,768]{1,0:T(8,128)} fusion(bf16[3136,768]{0,1:T(8,128)(2,1)} %all-gather.5.cloned.1.call-done, bf16[768,768]{1,0:T(8,128)(2,1)} %all-gather.7.cloned.1.call-done), kind=kOutput, calls=%fused_computation.92 | convolution fusion | flops 3699376128 | bytes 15630336 | tf_op jit(solution)/shard_map/dot_general | solution.py:108
  171.9 14.6 %all-gather.9.cloned.1.call-done = bf16[768,768]{0,1:T(8,128)(2,1)} async-done(((bf16[768,96]{0,1:T(8,128)(2,1)}), bf16[768,768]{0,1:T(8,128)(2,1)}) %all-gather.9.cloned.1.call-update) | async-done | bytes 1179664 | tf_op jit(solution)/shard_map/all_gather | solution.py:102
  186.5 10.6 %convolution_convert_fusion.1 = bf16[3136,768]{0,1:T(8,128)(2,1)} fusion(bf16[768,768]{0,1:T(8,128)(2,1)} %all-gather.9.cloned.1.call-done, f32[3136,768]{1,0:T(8,128)} %fusion.40, f32[768]{0:T(1024)S(1)} %dynamic_slice.12), kind=kOutput, calls=%fused_computation.14 | convolution fusion | flops 3725869056 | bytes 15633408 | tf_op jit(solution)/shard_map/dot_general | solution.py:112
  197.6 83.0 %all-gather.11.cloned.1.call-done = bf16[3136,768]{0,1:T(8,128)(2,1)} async-done(((bf16[3136,192]{0,1:T(8,128)(2,1)}), bf16[3136,768]{0,1:T(8,128)(2,1)}) %all-gather.11.cloned.1.call-update) | async-done | bytes 4816912 | tf_op jit(solution)/shard_map/all_gather | solution.py:45
  280.6 15.2 %convert_reduce_fusion = (f32[768]{0:T(1024)S(1)}, bf16[3136,768]{1,0:T(8,128)(2,1)S(1)}) fusion(f32[3136,768]{1,0:T(8,128)} %fusion.40, f32[768]{0:T(1024)S(1)} %dynamic_slice.12, bf16[3136,768]{0,1:T(8,128)(2,1)} %all-gather.11.cloned.1.call-done, bf16[768,768]{0,1:T(8,128)(2,1)} %all-gather.9.cloned.1.call-done), kind=kOutput, calls=%fused_computation.9 | convolution fusion | flops 3754769664 | bytes 20453376 | tf_op jit(solution)/shard_map/dot_general | solution.py:116
  298.0 5.9 convolution_convert_fusion
  303.9 10.6 %convolution_convert_fusion.2 = bf16[768,768]{0,1:T(8,128)(2,1)} fusion(bf16[3136,768]{0,1:T(8,128)(2,1)} %all-gather.11.cloned.1.call-done, f32[3136,768]{1,0:T(8,128)} %fusion.40, f32[768]{0:T(1024)S(1)} %dynamic_slice.12), kind=kOutput, calls=%fused_computation.49 | convolution fusion | flops 3724050432 | bytes 15633408 | tf_op jit(solution)/shard_map/dot_general | solution.py:117
  318.9 9.1 %convolution_convert_fusion.3 = bf16[768,768]{1,0:T(8,128)(2,1)} fusion(bf16[3136,768]{0,1:T(8,128)(2,1)} %all-gather.5.cloned.1.call-done, bf16[3136,768]{1,0:T(8,128)(2,1)} %copy-done.29), kind=kOutput, calls=%fused_computation.50 | convolution fusion | flops 3699965952 | bytes 10813440 | tf_op jit(solution)/shard_map/dot_general | solution.py:119
  328.0 7.7 %all-to-all-done.1 = bf16[8,768,96]{1,2,0:T(8,128)(2,1)} async-done(((bf16[8,768,96]{1,2,0:T(8,128)(2,1)}), bf16[8,768,96]{1,2,0:T(8,128)(2,1)}, u32[]{:S(2)}, u32[]{:S(2)}) %all-to-all-start.1) | async-done | bytes 1179680 | tf_op jit(solution)/shard_map/all_to_all | solution.py:21
  359.0 10.6 %reduce-scatter.3.cloned.1.call-done = bf16[3136,192]{0,1:T(8,128)(2,1)} async-done(((bf16[3136,768]{0,1:T(8,128)(2,1)}), bf16[3136,192]{0,1:T(8,128)(2,1)}) %reduce-scatter.3.cloned.1.call-update) | async-done | bytes 1204240 | tf_op jit(solution)/shard_map/reduce_scatter | solution.py:49
  371.2 5.7 reshape.138
  376.9 84.1 %reduce-scatter.5.cloned.1.call-done = bf16[3136,192]{0,1:T(8,128)(2,1)} async-done(((bf16[3136,768]{0,1:T(8,128)(2,1)}), bf16[3136,192]{0,1:T(8,128)(2,1)}) %reduce-scatter.5.cloned.1.call-update) | async-done | bytes 1204240 | tf_op jit(solution)/shard_map/reduce_scatter | solution.py:49
  462.7 5.8 reshape.130
  473.8 18.5 %all-reduce.3 = (f32[16,196]{1,0:T(8,128)S(1)}, f32[16,196]{1,0:T(8,128)S(1)}) all-reduce(f32[16,196]{1,0:T(8,128)S(1)} %get-tuple-element.18, f32[16,196]{1,0:T(8,128)S(1)} %reduce_sum.187), channel_id=1, replica_groups=mesh['dp'=8,'tp'=4] {'tp'}, use_global_device_ids=true, to_apply=%region_13.0 | all-reduce | flops 6272 | bytes 50176 | tf_op jit(solution)/shard_map/psum | solution.py:33
  492.4 8.5 %convert_reduce_fusion.3 = (f32[196]{0:T(256)}, f32[16,196,192]{1,2,0:T(8,128)S(1)}, bf16[16,196,192]{1,2,0:T(8,128)(2,1)}) fusion(f32[16,196,192]{1,2,0:T(8,128)} %copy.76, f32[16,196]{1,0:T(8,128)S(1)} %get-tuple-element.39, f32[16,196,192]{1,2,0:T(8,128)} %copy-done.2, f32[16,196]{1,0:T(8,128)S(1)} %get-tuple-element.55, ...), kind=kLoop, calls=%fused_computation.32 | loop fusion | flops 8429372 | bytes 13298192 | tf_op jit(solution)/shard_map/reduce_sum | solution.py:139
  500.9 6.2 convolution_bitcast_fusion
  507.1 5.5 convert_reduce_fusion.1
  534.5 18.6 %all-reduce.2 = (f32[16,196]{1,0:T(8,128)S(1)}, f32[16,196]{1,0:T(8,128)S(1)}, f32[2,768]{1,0:T(2,128)S(1)}, f32[384]{0:T(512)S(1)}, f32[196]{0:T(256)S(1)}, /*index=5*/f32[3072]{0:T(1024)S(1)}, f32[768]{0:T(1024)S(1)}) all-reduce(f32[16,196]{1,0:T(8,128)S(1)} %get-tuple-element.16, ...), channel_id=1, replica_groups=mesh['dp'=8,'tp'=4] {'tp'}, use_global_device_ids=true, to_apply=%region_17.0 | all-reduce | flops 12228 | bytes 97824 | tf_op jit(solution)/shard_map/psum | solution.py:33
  553.2 25.5 %all-reduce.12.cloned.1.call-done = (f32[64,2,768]{2,0,1:T(8,128)}, f32[196,384]{1,0:T(8,128)}, f32[384,196]{0,1:T(8,128)}) async-done(((f32[64,2,768]{2,0,1:T(8,128)}, f32[196,384]{1,0:T(8,128)}, f32[384,196]{0,1:T(8,128)}), (f32[64,2,768]{2,0,1:T(8,128)}, f32[196,384]{1,0:T(8,128)}, f32[384,196]{0,1:T(8,128)})) %all-reduce.12.cloned.1.call-update) | async-done | bytes 995344 | tf_op jit(solution)/shard_map/psum | solution.py:154
  589.2 24.9 %all-reduce = (f32[2,768]{1,0:T(2,128)S(1)}, f32[384]{0:T(512)}, f32[196]{0:T(256)}, f32[3072]{0:T(1024)}, f32[768]{0:T(1024)}) all-reduce(f32[2,768]{1,0:T(2,128)S(1)} %get-tuple-element.34, f32[384]{0:T(512)S(1)} %get-tuple-element.35, f32[196]{0:T(256)S(1)} %get-tuple-element.36, ...), channel_id=1, replica_groups=mesh['dp'=8,'tp'=4] {'dp'}, use_global_device_ids=true, to_apply=%region_26.0 | all-reduce | flops 5956 | bytes 47648 | tf_op jit(solution)/shard_map/psum | solution.py:153
  614.2 24.6 %all-reduce.10.cloned.1.call-done = (f32[64,2,768]{2,0,1:T(8,128)}, f32[196,384]{1,0:T(8,128)}, f32[384,196]{0,1:T(8,128)}) async-done(((f32[64,2,768]{2,0,1:T(8,128)}, f32[196,384]{1,0:T(8,128)}, f32[384,196]{0,1:T(8,128)}), (f32[64,2,768]{2,0,1:T(8,128)}, f32[196,384]{1,0:T(8,128)}, f32[384,196]{0,1:T(8,128)})) %all-reduce.10.cloned.1.call-update) | async-done | bytes 995344 | tf_op jit(solution)/shard_map/psum | solution.py:153
  (149 shorter events, 110.3 us)
Async XLA Ops:
  7.2 69.9 %all-gather.7.cloned.1.call-start = ((), (), s32[]{:S(2)}) async-start(), calls=%async_computation.5 | async-start | bytes 1327104 | tf_op jit(solution)/shard_map/all_gather | solution.py:101
  8.9 152.6 %all-gather.5.cloned.1.call-start = ((), (), s32[]{:S(2)}) async-start(), calls=%async_computation.4 | async-start | bytes 6144000 | tf_op jit(solution)/shard_map/all_gather | solution.py:45
  12.9 25.4 %copy-start.16 = (f32[192]{0:T(256)S(1)}, f32[192]{0:T(256)}, u32[]{:S(2)}) copy-start(f32[192]{0:T(256)} %param.16) | copy-start | bytes 2308
  16.1 25.8 %copy-start.7 = (f32[196,384]{1,0:T(8,128)S(1)}, f32[196,384]{1,0:T(8,128)}, u32[]{:S(2)}) copy-start(f32[196,384]{1,0:T(8,128)} %param.18) | copy-start | bytes 903172
  43.9 18.4 %copy-start.15 = (f32[192]{0:T(256)S(1)}, f32[192]{0:T(256)}, u32[]{:S(2)}) copy-start(f32[192]{0:T(256)} %param.22) | copy-start | bytes 2308
  43.9 18.4 %copy-start.21 = (f32[192]{0:T(256)S(1)}, f32[192]{0:T(256)}, u32[]{:S(2)}) copy-start(f32[192]{0:T(256)} %param.23) | copy-start | bytes 2308
  46.4 18.5 %copy-start.2 = (f32[16,196,192]{1,2,0:T(8,128)}, f32[16,196,192]{1,2,0:T(8,128)S(1)}, u32[]{:S(2)}) copy-start(f32[16,196,192]{1,2,0:T(8,128)S(1)} %get-tuple-element.63) | copy-start | bytes 7225348
  69.3 117.2 %all-gather.9.cloned.1.call-start = ((), (), s32[]{:S(2)}) async-start(), calls=%async_computation.6 | async-start | bytes 1327104 | tf_op jit(solution)/shard_map/all_gather | solution.py:102
  71.0 209.6 %all-gather.11.cloned.1.call-start = ((), (), s32[]{:S(2)}) async-start(), calls=%async_computation.8 | async-start | bytes 6144000 | tf_op jit(solution)/shard_map/all_gather | solution.py:45
  76.1 293.6 %reduce-scatter.3.cloned.1.call-start = ((), (), s32[]{:S(2)}) async-start(), calls=%async_computation.7 | async-start | bytes 6144000 | tf_op jit(solution)/shard_map/reduce_scatter | solution.py:49
  197.1 100.9 %copy-start.23 = (bf16[768,768]{1,0:T(8,128)(2,1)S(1)}, bf16[768,768]{1,0:T(8,128)(2,1)}, u32[]{:S(2)}) copy-start(bf16[768,768]{1,0:T(8,128)(2,1)} %all-gather.7.cloned.1.call-done) | copy-start | bytes 3538948
  197.1 263.8 %reduce-scatter.5.cloned.1.call-start = ((), (), s32[]{:S(2)}) async-start(), calls=%async_computation.9 | async-start | bytes 6144000 | tf_op jit(solution)/shard_map/reduce_scatter | solution.py:49
  314.5 21.3 %all-to-all-start.1 = ((bf16[8,768,96]{1,2,0:T(8,128)(2,1)}), bf16[8,768,96]{1,2,0:T(8,128)(2,1)}, u32[]{:S(2)}, u32[]{:S(2)}) async-start(bf16[8,768,96]{1,2,0:T(8,128)(2,1)} %bitcast.18), calls=%async_computation.3 | async-start | bytes 2359296 | tf_op jit(solution)/shard_map/all_to_all | solution.py:21
  328.0 12.1 %copy-start.5 = (bf16[16,1,37632]{2,0,1:T(8,128)(2,1)S(1)}, bf16[16,1,37632]{2,0,1:T(8,128)(2,1)}, u32[]{:S(2)}) copy-start(bf16[16,1,37632]{2,0,1:T(8,128)(2,1)} %param.29) | copy-start | bytes 3612676
  335.8 21.1 %all-to-all-start = ((bf16[8,96,768]{2,1,0:T(8,128)(2,1)}), bf16[8,96,768]{2,1,0:T(8,128)(2,1)}, u32[]{:S(2)}, u32[]{:S(2)}) async-start(bf16[8,96,768]{2,1,0:T(8,128)(2,1)} %bitcast.81), calls=%async_computation.2 | async-start | bytes 2359296 | tf_op jit(solution)/shard_map/all_to_all | solution.py:21
  340.0 238.6 %all-reduce.12.cloned.1.call-start = ((), (), s32[]{:S(2)}) async-start(), calls=%async_computation.11 | async-start | bytes 2015232 | tf_op jit(solution)/shard_map/psum | solution.py:154
  492.3 8.6 %copy-start.27 = (f32[384]{0:T(512)S(1)}, f32[384]{0:T(512)}, u32[]{:S(2)}) copy-start(f32[384]{0:T(512)} %param.19) | copy-start | bytes 4612
  492.4 14.7 %slice-start = ((s8[4718592]{0:T(1024)(128)(4,1)}), s8[4194304]{0:T(1024)(128)(4,1)S(1)}, s32[]{:S(2)}) async-start(s8[4718592]{0:T(1024)(128)(4,1)} %bitcast.79), calls=%async_computation.12 | async-start | bytes 8388608
  519.4 7.4 %copy-start.1 = (f32[16,196,192]{1,2,0:T(8,128)S(1)}, f32[16,196,192]{1,2,0:T(8,128)}, u32[]{:S(2)}) copy-start(f32[16,196,192]{1,2,0:T(8,128)} %copy.70) | copy-start | bytes 7225348
  519.4 7.4 %copy-start.9 = (f32[16,196]{1,0:T(8,128)S(1)}, f32[16,196]{1,0:T(8,128)}, u32[]{:S(2)}) copy-start(f32[16,196]{1,0:T(8,128)} %copy-done.8) | copy-start | bytes 37636
  519.4 7.4 %copy-start.11 = (f32[16,196]{1,0:T(8,128)S(1)}, f32[16,196]{1,0:T(8,128)}, u32[]{:S(2)}) copy-start(f32[16,196]{1,0:T(8,128)} %copy-done.10) | copy-start | bytes 37636
  519.4 7.4 %copy-start.17 = (f32[192]{0:T(256)S(1)}, f32[192]{0:T(256)}, u32[]{:S(2)}) copy-start(f32[192]{0:T(256)} %param.16) | copy-start | bytes 2308
  526.7 112.1 %all-reduce.10.cloned.1.call-start = ((), (), s32[]{:S(2)}) async-start(), calls=%async_computation.10 | async-start | bytes 2015232 | tf_op jit(solution)/shard_map/psum | solution.py:153
  532.1 46.5 %copy-start.18 = (f32[192]{0:T(256)S(1)}, f32[192]{0:T(256)}, u32[]{:S(2)}) copy-start(f32[192]{0:T(256)} %param.16) | copy-start | bytes 2308
  (18 other events, 52.2 us)
Sparse Core Ops, SparseCore 0:
  10.5 26.7 all-gather.6
  69.4 92.0 all-gather.4
  164.0 22.4 all-gather.8
  187.9 92.6 all-gather.10
  282.8 86.8 reduce-scatter.2
  372.0 88.9 reduce-scatter.4
  526.8 51.7 all-reduce.11
  582.6 56.2 all-reduce.9
